TPU v7x, 256 devices: a whole 4x4x8 slice. The times are simulated.
256 devices in a mesh: pair: 8 (over y_lo, x), feat: 32 (over y_hi, z, core).
Axes of the slice: x: 4, y: 4 (y_hi: 2, y_lo: 2; y = y_hi * 2 + y_lo), z: 8, core: 2. Of those that a mesh axis runs over, the one named last changes fastest.
Arguments:
- decoder: float32 [8, 16384, 2048], P('pair', 'feat'), may hold values from -0.3125 to 0.3125
- pair_map: int32 [8, 2], P('pair'), may hold values from 0 to 3, as said below
- indices: int32 [3, 256, 128], replicated, may hold values from 0 to 16383, as said below
- values: float32 [3, 256, 128], replicated, may hold values from 0.2 to 3
- target: float32 [3, 256, 2048], P(None, ('pair', 'feat')), may hold values from -6 to 6
Outputs:
- recon: bfloat16 [3, 256, 2048], P(None, ('pair', 'feat'))
- dec_grad: float32 [8, 16384, 2048], P('pair', 'feat')
- feat_grad: float32 [3, 256, 128], P(None, ('pair', 'feat'))
Inputs may be any that keep to these rules, and one draw needn't show every extreme that they name: `pair_map`: each pair (s, t) of layers with s <= t < 3 stands in exactly one row as (s, t); every other row is (3, 3), an empty slot. For each layer and token the 128 indices are distinct.
All inputs are finite; a program needn't handle non-finite values.
Results may differ from a plain program's by a relative error of at most 0.0027.
Values may be sent and summed in bfloat16 or wider, within the bound.
A program may use at most 128 MiB of HBM per device.

v0:
```python
import jax
import jax.numpy as jnp
from jax import lax
from jax.sharding import PartitionSpec as P


def pick_layer(stack, chosen_layer):
    layer_ids = jnp.arange(stack.shape[0], dtype=jnp.int32)[:, None, None]
    return jnp.sum(jnp.where(layer_ids == chosen_layer, stack, jnp.zeros_like(stack)), axis=0)


def body(decoder, pair_map, indices, values, target):
    slot_count, block_width, model_width = decoder.shape
    layers = indices.shape[0]
    first_feature = lax.axis_index("feat") * block_width
    columns = jnp.arange(block_width, dtype=jnp.int32)
    sources = pair_map[:, 0]
    goals = pair_map[:, 1]
    slot_index = 0
    picked = jnp.minimum(sources[slot_index], layers - 1)
    local_ids = pick_layer(indices, picked) - first_feature
    weights = pick_layer(values, picked)
    matches = (local_ids[:, :, None] == columns).astype(jnp.float32)
    active = jnp.einsum(
        "tk,tkf->tf",
        weights,
        matches,
        precision=lax.Precision.HIGHEST,
        preferred_element_type=jnp.float32,
    )
    product = jnp.dot(
        active,
        decoder[slot_index],
        precision=lax.Precision.HIGHEST,
        preferred_element_type=jnp.float32,
    )
    local_list = [local_ids]
    active_list = [active]
    product_list = [product]
    stacked = jnp.stack(product_list)
    choose_goal = jax.nn.one_hot(goals, layers, dtype=jnp.float32)
    choose_narrow = choose_goal.astype(jnp.bfloat16)
    layer_term = jnp.einsum(
        "jl,jtd->ltd",
        choose_goal,
        stacked,
        precision=lax.Precision.HIGHEST,
        preferred_element_type=jnp.float32,
    )
    shares = lax.psum_scatter(layer_term, ("pair", "feat"), scatter_dimension=1, tiled=True)
    error_share = (shares - target).astype(jnp.bfloat16)
    error_full = lax.all_gather(error_share, ("pair", "feat"), axis=1, tiled=True)
    slot_errors = jnp.einsum(
        "jl,ltd->jtd", choose_narrow, error_full, preferred_element_type=jnp.float32
    ).astype(jnp.bfloat16)
    recon = shares.astype(jnp.bfloat16)
    slot_index = 0
    slot_error = slot_errors[slot_index].astype(jnp.float32)
    tile_grad = jnp.dot(
        active_list[slot_index].T,
        slot_error,
        precision=lax.Precision.HIGHEST,
        preferred_element_type=jnp.float32,
    )
    grad_list = [tile_grad]
    back = jnp.dot(
        slot_error,
        decoder[slot_index].T,
        precision=lax.Precision.HIGHEST,
        preferred_element_type=jnp.float32,
    )
    matches = (local_list[slot_index][:, :, None] == columns).astype(jnp.float32)
    picked_grad = jnp.einsum(
        "tkf,tf->tk",
        matches,
        back,
        precision=lax.Precision.HIGHEST,
        preferred_element_type=jnp.float32,
    )
    choose_source = jax.nn.one_hot(sources[slot_index], layers, dtype=jnp.float32)
    feature_term = choose_source[:, None, None] * picked_grad[None]
    dec_grad = jnp.stack(grad_list)
    feat_grad = lax.psum_scatter(feature_term, ("pair", "feat"), scatter_dimension=1, tiled=True)
    return (recon, dec_grad, feat_grad)


def solution(mesh):
    in_specs = (P("pair", "feat", None), P("pair", None), P(), P(), P(None, ("pair", "feat"), None))
    out_specs = (
        P(None, ("pair", "feat"), None),
        P("pair", "feat", None),
        P(None, ("pair", "feat"), None),
    )
    return jax.shard_map(body, mesh=mesh, in_specs=in_specs, out_specs=out_specs, check_vma=False)
```

profile of v0, /device:TPU:2, one launch (start us, length us, event | category | flops | bytes accessed | tf_op | source)
XLA Modules:
  0.0 1048.4 jit_solution(10654120748516346442)
XLA Ops:
  7.2 0.0 all-reduce.5.cloned.1.call-start
  7.2 1.3 fusion.18
  9.2 1.1 select_reduce_fusion
  10.3 1.1 select_reduce_fusion.1
  11.4 0.7 compare_convert_fusion.1
  12.1 0.0 copy-start
  12.1 23.2 %fusion.1 = f32[256,1,512]{2,1,0:T(1,128)S(1)} fusion(f32[256,128,1]{1,2,0:T(1,128)S(1)} %bitcast.32, s32[256,128]{1,0:T(8,128)S(1)} %broadcast_subtract_fusion), kind=kOutput, calls=%fused_computation.2 | convolution fusion | flops 218103808 | bytes 786432 | tf_op jit(solution)/shard_map/tk,tkf->tf/dot_general | solution.py:24
  35.3 0.0 copy-done
  35.3 3.7 fusion.6
  39.0 5.7 broadcast_multiply_fusion
  44.7 0.0 copy-start.2
  44.7 0.0 all-reduce.5.cloned.1.call-update
  44.7 0.0 all-gather.2.cloned.1.call-start
  44.8 283.0 %all-reduce.5.cloned.1.call-done = f32[3,256,2048]{2,0,1:T(4,128)} async-done(((f32[3,256,2048]{2,0,1:T(4,128)}), f32[3,256,2048]{2,0,1:T(4,128)}) %all-reduce.5.cloned.1.call-update) | async-done | bytes 6291472
  327.8 0.0 copy-done.2
  327.8 1.4 fusion.16
  329.2 0.0 all-gather.2.cloned.1.call-update
  329.2 0.2 all-reduce.7.cloned.1.call-start
  329.5 0.7 compare_convert_fusion
  330.1 1.4 dynamic-slice_convert_fusion
  331.5 414.0 %all-gather.2.cloned.1.call-done = bf16[3,256,2048]{2,0,1:T(4,128)(2,1)} async-done(((bf16[3,1,2048]{2,0,1:T(4,128)(2,1)}), bf16[3,256,2048]{2,0,1:T(4,128)(2,1)}) %all-gather.2.cloned.1.call-update) | async-done | bytes 3145744 | tf_op jit(solution)/shard_map/all_gather | solution.py:52
  745.5 0.0 copy-start.1
  745.5 5.5 fusion.17
  750.9 0.0 copy-done.1
  750.9 2.6 fusion.8
  753.5 32.3 %fusion = f32[256,1,128]{2,1,0:T(1,128)S(1)} fusion(s32[256,128]{1,0:T(8,128)S(1)} %broadcast_subtract_fusion, f32[256,512,1]{1,0,2:T(8,128)S(1)} %fusion.8), kind=kOutput, calls=%fused_computation.1 | convolution fusion | flops 218103808 | bytes 786432 | tf_op jit(solution)/shard_map/tkf,tf->tk/dot_general | solution.py:73
  785.9 1.0 broadcast_multiply_fusion.1
  786.8 0.0 all-reduce.7.cloned.1.call-update
  786.9 4.1 convolution_bitcast_fusion
  791.0 249.6 %all-reduce.7.cloned.1.call-done = f32[3,256,128]{2,0,1:T(4,128)} async-done(((f32[3,256,128]{2,0,1:T(4,128)}), f32[3,256,128]{2,0,1:T(4,128)}) %all-reduce.7.cloned.1.call-update) | async-done | bytes 393232
  1040.6 0.7 constant_dynamic-slice_fusion
  1041.3 0.6 copy.10
  (2 shorter events, 0.0 us)
Async XLA Ops:
  7.2 320.7 %all-reduce.5.cloned.1.call-start = ((), (), s32[]{:S(2)}) async-start(), calls=%async_computation.1 | async-start | bytes 16777216
  12.1 23.2 %copy-start = (f32[1,512,2048]{2,1,0:T(8,128)S(1)}, f32[1,512,2048]{2,1,0:T(8,128)}, u32[]{:S(2)}) copy-start(f32[1,512,2048]{2,1,0:T(8,128)} %param.5) | copy-start | bytes 12582916
  44.7 283.1 %copy-start.2 = (f32[3,1,2048]{2,1,0:T(1,128)S(1)}, f32[3,1,2048]{2,1,0:T(1,128)}, u32[]{:S(2)}) copy-start(f32[3,1,2048]{2,1,0:T(1,128)} %param.9) | copy-start | bytes 73732
  44.7 700.7 %all-gather.2.cloned.1.call-start = ((), (), s32[]{:S(2)}) async-start(), calls=%async_computation | async-start | bytes 4210688 | tf_op jit(solution)/shard_map/all_gather | solution.py:52
  329.2 711.3 %all-reduce.7.cloned.1.call-start = ((), (), s32[]{:S(2)}) async-start(), calls=%async_computation.2 | async-start | bytes 1048576
  745.5 5.5 copy-start.1
Sparse Core Ops, SparseCore 0:
  44.8 282.9 all-reduce.4
  330.3 415.1 all-gather.1
  787.0 253.5 all-reduce.6
where the time goes:
time: 1050 us
  waiting for transfers between devices  947 us (90%)
  matrix products  71.4 us (7%)
  between operations  14.5 us (1%)
  other arithmetic  11.5 us (1%)
    unnamed x5, waiting for transfers between devices  533 us
    all_gather x1, waiting for transfers between devices, body(): lax.all_gather(error_share, ('pair', 'feat'), axis=1, tiled=True)  414 us
    dot_general x1, matrix products, body(): jnp.einsum('tkf,tf->tk', matches, back, precision=lax.Precision.HIGHEST,...  32.3 us
    dot_general x1, matrix products, body(): jnp.einsum('tk,tkf->tf', weights, matches, precision=lax.Precision.HIGHES...  23.2 us
  transfers between devices with their start and end apart: 3, of which 3 were waited for; matrix products, arithmetic and copies ran while one was open for 1% of the time, Pallas kernels for 0%

commit v1 on v0

--- a/solution.py
+++ b/solution.py
@@ -49,7 +49,15 @@
     )
     shares = lax.psum_scatter(layer_term, ("pair", "feat"), scatter_dimension=1, tiled=True)
     error_share = (shares - target).astype(jnp.bfloat16)
-    error_full = lax.all_gather(error_share, ("pair", "feat"), axis=1, tiled=True)
+    error_full = jnp.concatenate(
+        jax.lax.all_to_all(
+            jnp.stack([error_share] * jax.lax.axis_size(("pair", "feat")), 0),
+            ("pair", "feat"),
+            0,
+            0,
+        ),
+        1,
+    )
     slot_errors = jnp.einsum(
         "jl,ltd->jtd", choose_narrow, error_full, preferred_element_type=jnp.float32
     ).astype(jnp.bfloat16)

time: 1050 us -> 744 us (0.71)
  waiting for transfers between devices: 947 us -> 624 us
  starting transfers between devices: 0.3 us -> 11.8 us
    all_gather x1 -> x0, waiting for transfers between devices: 414 us -> none  [body(): lax.all_gather(error_share, ('pair', 'feat'), axis=1, tiled=True)]
    all_to_all x0 -> x1, waiting for transfers between devices: none -> 91.9 us  [body(): jax.lax.all_to_all(jnp.stack([error_share] * jax.lax.axis_size(('pair', '...]
    all_to_all x0 -> x1, starting transfers between devices: none -> 11.5 us  [body(): jax.lax.all_to_all(jnp.stack([error_share] * jax.lax.axis_size(('pair', '...]
    unnamed x5 -> x4, waiting for transfers between devices: 533 us -> 532 us
where the time goes in v1:
time: 744 us
  waiting for transfers between devices  624 us (84%)
  matrix products  69.8 us (9%)
  between operations  14.8 us (2%)
  local copies, waits for them, and re-layouts  12.5 us (2%)
  starting transfers between devices  11.8 us (2%)
  other arithmetic  10.9 us (1%)
    unnamed x4, waiting for transfers between devices  532 us
    all_to_all x1, waiting for transfers between devices, body(): jax.lax.all_to_all(jnp.stack([error_share] * jax.lax.axis_size(('pair', '...  91.9 us
    dot_general x1, matrix products, body(): jnp.einsum('tkf,tf->tk', matches, back, precision=lax.Precision.HIGHEST,...  32.3 us
    dot_general x1, matrix products, body(): jnp.einsum('tk,tkf->tf', weights, matches, precision=lax.Precision.HIGHES...  23.2 us
  transfers between devices with their start and end apart: 3, of which 3 were waited for; matrix products, arithmetic and copies ran while one was open for 1% of the time, Pallas kernels for 0%

profile of v1, /device:TPU:2, one launch (start us, length us, event | category | flops | bytes accessed | tf_op | source)
XLA Modules:
  0.0 744.0 jit_solution(3360325042315136653)
XLA Ops:
  7.2 0.0 all-reduce.5.cloned.1.call-start
  7.2 1.3 fusion.25
  9.2 1.1 select_reduce_fusion.1
  10.3 1.1 select_reduce_fusion
  11.4 0.7 compare_convert_fusion.2
  12.1 0.0 copy-start
  12.1 23.2 %fusion.1 = f32[256,1,512]{2,1,0:T(1,128)S(1)} fusion(f32[256,128,1]{1,2,0:T(1,128)S(1)} %bitcast.41, s32[256,128]{1,0:T(8,128)S(1)} %broadcast_subtract_fusion), kind=kOutput, calls=%fused_computation.2 | convolution fusion | flops 218103808 | bytes 786432 | tf_op jit(solution)/shard_map/tk,tkf->tf/dot_general | solution.py:24
  35.3 0.0 copy-done
  35.3 3.7 fusion.6
  39.0 5.7 broadcast_multiply_fusion
  44.7 0.0 copy-start.2
  44.7 0.0 all-reduce.5.cloned.1.call-update
  44.7 283.1 %all-reduce.5.cloned.1.call-done = f32[3,256,2048]{2,0,1:T(4,128)} async-done(((f32[3,256,2048]{2,0,1:T(4,128)}), f32[3,256,2048]{2,0,1:T(4,128)}) %all-reduce.5.cloned.1.call-update) | async-done | bytes 6291472
  327.8 0.0 copy-done.2
  327.8 0.8 fusion.19
  328.6 4.1 stack.4
  332.7 11.5 %all-to-all-start = ((bf16[256,3,1,2048]{3,1,2,0:T(4,128)(2,1)}), bf16[256,3,1,2048]{3,1,2,0:T(4,128)(2,1)}, u32[]{:S(2)}, u32[]{:S(2)}) async-start(bf16[256,3,1,2048]{3,1,2,0:T(4,128)(2,1)} %stack.4), calls=%async_computation | async-start | bytes 8388608 | tf_op jit(solution)/shard_map/all_to_all | solution.py:53
  344.3 0.2 all-reduce.7.cloned.1.call-start
  344.5 0.7 compare_convert_fusion
  345.2 1.4 dynamic-slice_convert_fusion
  346.6 91.9 %all-to-all-done = bf16[256,3,1,2048]{3,1,2,0:T(4,128)(2,1)} async-done(((bf16[256,3,1,2048]{3,1,2,0:T(4,128)(2,1)}), bf16[256,3,1,2048]{3,1,2,0:T(4,128)(2,1)}, u32[]{:S(2)}, u32[]{:S(2)}) %all-to-all-start) | async-done | bytes 3145760 | tf_op jit(solution)/shard_map/all_to_all | solution.py:53
  438.5 4.5 copy.41
  442.9 0.0 copy-start.1
  442.9 3.8 fusion.8
  446.7 0.0 copy-done.1
  446.7 2.6 fusion.10
  449.3 32.3 %fusion = f32[256,1,128]{2,1,0:T(1,128)S(1)} fusion(s32[256,128]{1,0:T(8,128)S(1)} %broadcast_subtract_fusion, f32[256,512,1]{1,0,2:T(8,128)S(1)} %fusion.10), kind=kOutput, calls=%fused_computation.1 | convolution fusion | flops 218103808 | bytes 786432 | tf_op jit(solution)/shard_map/tkf,tf->tk/dot_general | solution.py:81
  481.7 1.0 broadcast_multiply_fusion.1
  482.7 0.0 all-reduce.7.cloned.1.call-update
  482.7 4.1 convolution_bitcast_fusion
  486.8 249.1 %all-reduce.7.cloned.1.call-done = f32[3,256,128]{2,0,1:T(4,128)} async-done(((f32[3,256,128]{2,0,1:T(4,128)}), f32[3,256,128]{2,0,1:T(4,128)}) %all-reduce.7.cloned.1.call-update) | async-done | bytes 393232
  735.9 0.7 constant_dynamic-slice_fusion
  736.6 0.6 copy.12
  (2 shorter events, 0.0 us)
Async XLA Ops:
  7.2 320.7 %all-reduce.5.cloned.1.call-start = ((), (), s32[]{:S(2)}) async-start(), calls=%async_computation.1 | async-start | bytes 16777216
  12.1 23.2 %copy-start = (f32[1,512,2048]{2,1,0:T(8,128)S(1)}, f32[1,512,2048]{2,1,0:T(8,128)}, u32[]{:S(2)}) copy-start(f32[1,512,2048]{2,1,0:T(8,128)} %param.5) | copy-start | bytes 12582916
  44.7 283.1 %copy-start.2 = (f32[3,1,2048]{2,1,0:T(1,128)S(1)}, f32[3,1,2048]{2,1,0:T(1,128)}, u32[]{:S(2)}) copy-start(f32[3,1,2048]{2,1,0:T(1,128)} %param.9) | copy-start | bytes 73732
  332.7 105.7 %all-to-all-start = ((bf16[256,3,1,2048]{3,1,2,0:T(4,128)(2,1)}), bf16[256,3,1,2048]{3,1,2,0:T(4,128)(2,1)}, u32[]{:S(2)}, u32[]{:S(2)}) async-start(bf16[256,3,1,2048]{3,1,2,0:T(4,128)(2,1)} %stack.4), calls=%async_computation | async-start | bytes 8388608 | tf_op jit(solution)/shard_map/all_to_all | solution.py:53
  344.3 391.6 %all-reduce.7.cloned.1.call-start = ((), (), s32[]{:S(2)}) async-start(), calls=%async_computation.2 | async-start | bytes 1048576
  442.9 3.8 copy-start.1
Sparse Core Ops, SparseCore 0:
  44.8 282.9 all-reduce.4
  482.8 253.0 all-reduce.6
